TPU v7x, 512 devices: a whole 4x4x16 slice. The times are simulated.
512 devices in a mesh: gz: 32 (over y, z_hi, core), gy: 16 (over z_lo, x).
Axes of the slice: x: 4, y: 4, z: 16 (z_hi: 4, z_lo: 4; z = z_hi * 4 + z_lo), core: 2. Of those that a mesh axis runs over, the one named last changes fastest.
Arguments:
- features: bfloat16 [16, 128, 128, 128], P(None, 'gz', 'gy'), may hold values from -6 to 6
- labels: int32 [128, 128, 128], P('gz', 'gy'), may hold values from 0 to 1
- sign_map: int32 [128, 128, 128], P('gz', 'gy'), may hold values from 0 to 1
- conv_first: bfloat16 [16, 16, 3, 3, 3], replicated, may hold values from -0.3125 to 0.3125
- conv_second: bfloat16 [16, 16, 3, 3, 3], replicated, may hold values from -0.3125 to 0.3125
- speed_weight: float32 [16], replicated, may hold values from -1.5 to 1.5
Outputs:
- d_features: bfloat16 [16, 128, 128, 128], P(None, 'gz', 'gy')
- grad_first: float32 [16, 16, 3, 3, 3], replicated
- grad_second: float32 [16, 16, 3, 3, 3], replicated
- grad_speed: float32 [16], replicated
All inputs are finite; a program needn't handle non-finite values.
Results may differ from a plain program's by a relative error of at most 0.01.
Values may be sent and summed in bfloat16 or wider, within the bound.
No kernel may reach another device: no remote copies, remote signals or barrier semaphores. Data moves between devices by JAX's collectives and lax.ppermute only.
A program may use at most 128 MiB of HBM per device.

v0:
```python
import jax
import jax.numpy as jnp
from jax import lax
from jax.sharding import PartitionSpec as P

C = 16
STEPS = 4
time_step = 0.25
spread_rate = 0.5
slope_floor = 0.1
layout = ("NCDHW", "OIDHW", "NCDHW")


def extended(value, sides, width):
    for axis, dim in sides:
        size, length = (lax.axis_size(axis), value.shape[dim])
        up = [(i, (i + 1) % size) for i in range(size - 1)]
        down = [(j, i) for i, j in up]
        last = lax.slice_in_dim(value, length - width, length, axis=dim)
        initial = lax.slice_in_dim(value, 0, width, axis=dim)
        before = lax.ppermute(last, axis, up)
        after = lax.ppermute(initial, axis, down)
        value = jnp.concatenate([before, value, after], axis=dim)
    return value


def for_sending(value):
    return jax.tree.map(lambda a: a.astype(jnp.bfloat16) if a.dtype == jnp.float32 else a, value)


def from_behind(block, axis, distance):
    devices = range(lax.axis_size(axis))
    route = [(i - distance, i) for i in devices if i - distance in devices]
    return lax.ppermute(block, axis, route)


def front(padded, speed):
    grid = jnp.pad(padded, ((0, 0), (0, 0), (1, 1)))
    centre = grid[1:-1, 1:-1, 1:-1]
    up_z = grid[2:, 1:-1, 1:-1]
    low_z = grid[:-2, 1:-1, 1:-1]
    up_y = grid[1:-1, 2:, 1:-1]
    low_y = grid[1:-1, :-2, 1:-1]
    up_x = grid[1:-1, 1:-1, 2:]
    low_x = grid[1:-1, 1:-1, :-2]
    dif_z = (up_z - low_z) * 0.5
    dif_y = (up_y - low_y) * 0.5
    dif_x = (up_x - low_x) * 0.5
    slope = jnp.sqrt(dif_z * dif_z + dif_y * dif_y + dif_x * dif_x + slope_floor)
    laplace = up_z + low_z + up_y + low_y + up_x + low_x - 6.0 * centre
    return centre + time_step * (speed * slope + spread_rate * laplace)


def silu_slope(value):
    sig = jax.nn.sigmoid(value)
    return sig * (1.0 + value * (1.0 - sig))


def conv_halo(field):
    return extended(field, (("gz", 1), ("gy", 2)), 1)


def conv_local(padded, weight):
    grid = jnp.pad(padded, ((0, 0), (0, 0), (0, 0), (1, 1)))
    return lax.conv_general_dilated(
        grid[None],
        weight,
        (1, 1, 1),
        "VALID",
        dimension_numbers=layout,
        preferred_element_type=jnp.float32,
    )[0]


def flip_weight(weight):
    return jnp.flip(weight, (2, 3, 4)).transpose(1, 0, 2, 3, 4)


def weight_grad(padded, d_out):
    grid = jnp.pad(padded, ((0, 0), (0, 0), (0, 0), (1, 1)))
    d_weight = lax.conv_general_dilated(
        grid[:, None],
        d_out[:, None],
        (1, 1, 1),
        "VALID",
        dimension_numbers=layout,
        preferred_element_type=jnp.float32,
    )
    return d_weight.transpose(1, 0, 2, 3, 4)


def conv_back(weight, d_out):
    d_grid = lax.conv_general_dilated(
        d_out[None],
        flip_weight(weight),
        (1, 1, 1),
        ((2, 2), (2, 2), (2, 2)),
        dimension_numbers=layout,
        preferred_element_type=jnp.float32,
    )[0]
    return d_grid[..., 1:-1]


def fold_axis(grad, width, dim, which):
    inner = grad.shape[dim] - 2 * width
    lower = lax.slice_in_dim(grad, 0, width, axis=dim)
    upper = lax.slice_in_dim(grad, inner + width, inner + 2 * width, axis=dim)
    core = lax.slice_in_dim(grad, width, inner + width, axis=dim)
    if which == 0:
        from_below = from_behind(for_sending(upper), "gz", 1).astype(upper.dtype)
        from_above = from_behind(for_sending(lower), "gz", -1).astype(lower.dtype)
    else:
        from_below = from_behind(for_sending(upper), "gy", 1).astype(upper.dtype)
        from_above = from_behind(for_sending(lower), "gy", -1).astype(lower.dtype)
    head = [(0, 0)] * grad.ndim
    tail = [(0, 0)] * grad.ndim
    head[dim] = (0, inner - width)
    tail[dim] = (inner - width, 0)
    return core + jnp.pad(from_below, head) + jnp.pad(from_above, tail)


def fold_rims(grad, width, zdim):
    return fold_axis(fold_axis(grad, width, zdim, 0), width, zdim + 1, 1)


def input_grad(weight, d_out):
    return fold_rims(conv_back(weight, d_out), 1, 1)


def on_device(features, labels, sign_map, conv_first, conv_second, speed_weight):
    high = lax.Precision.HIGHEST
    feat_pad = conv_halo(features)
    act_first = conv_local(feat_pad, conv_first)
    hidden = jax.nn.silu(act_first).astype(jnp.bfloat16)
    hidden_pad = conv_halo(hidden)
    act_second = conv_local(hidden_pad, conv_second)
    top = jax.nn.silu(act_second)
    speed = jnp.tanh(jnp.einsum("c,czyx->zyx", speed_weight, top, precision=high))
    phi_start = 2.0 * sign_map.astype(jnp.float32) - 1.0
    target = labels.astype(jnp.float32)
    stored = []
    phi = phi_start
    for step in range(STEPS):
        padded = extended(phi, (("gz", 0), ("gy", 1)), 1)
        stored.append(padded)
        phi = front(padded, speed)
    d_phi = jax.nn.sigmoid(phi) - target
    d_speed = jnp.zeros_like(speed)
    for padded in reversed(stored):
        back = jax.vjp(front, padded, speed)[1]
        d_padded, d_part = back(d_phi)
        d_speed = d_speed + d_part
        d_phi = fold_rims(d_padded, 1, 0)
    d_pre = d_speed * (1.0 - speed * speed)
    raw_speed = jnp.einsum("zyx,czyx->c", d_pre, top, precision=high)
    d_second = (speed_weight[:, None, None, None] * d_pre[None] * silu_slope(act_second)).astype(
        jnp.bfloat16
    )
    raw_second = weight_grad(hidden_pad, d_second)
    d_hidden = input_grad(conv_second, d_second)
    d_first = (d_hidden * silu_slope(act_first)).astype(jnp.bfloat16)
    raw_first = weight_grad(feat_pad, d_first)
    d_feat = input_grad(conv_first, d_first)
    raw_first, raw_second, raw_speed = lax.psum((raw_first, raw_second, raw_speed), ("gz", "gy"))
    total = (
        jnp.sum(raw_first * raw_first)
        + jnp.sum(raw_second * raw_second)
        + jnp.sum(raw_speed * raw_speed)
    )
    count = 54.0 * C * C + C
    factor = 1.0 / jnp.maximum(jnp.sqrt(total) / jnp.sqrt(jnp.float32(count)), 1.0)
    return (
        d_feat.astype(jnp.bfloat16),
        raw_first * factor,
        raw_second * factor,
        raw_speed * factor,
    )


def solution(mesh):
    in_specs = (P(None, "gz", "gy", None), P("gz", "gy", None), P("gz", "gy", None), P(), P(), P())
    out_specs = (P(None, "gz", "gy", None), P(), P(), P())
    return jax.shard_map(
        on_device, mesh=mesh, in_specs=in_specs, out_specs=out_specs, check_vma=False
    )
```

profile of v0, /device:TPU:15, one launch (start us, length us, event | category | flops | bytes accessed | tf_op | source)
XLA Modules:
  0.0 515.8 jit_solution(8016700852686420210)
XLA Ops:
  1.5 9.4 %collective-permute-start = (bf16[16,1,8,128]{3,0,2,1:T(8,128)(2,1)S(1)}, bf16[16,1,8,128]{3,0,2,1:T(8,128)(2,1)S(1)}, u32[]{:S(2)}, u32[]{:S(2)}) collective-permute-start(bf16[16,1,8,128]{3,0,2,1:T(8,128)(2,1)S(1)} %copy.83), channel_id=1, source_target_pairs={{0,16},{16,32},{32,48},{48,64},{64,80},{80,96},{96,112},{112,128},... | collective-permute-start | bytes 98312 | tf_op jit(solution)/shard_map/ppermute | solution.py:21
  14.5 5.5 %collective-permute-done.1 = bf16[16,1,8,128]{3,0,2,1:T(8,128)(2,1)S(1)} collective-permute-done((bf16[16,1,8,128]{3,0,2,1:T(8,128)(2,1)S(1)}, bf16[16,1,8,128]{3,0,2,1:T(8,128)(2,1)S(1)}, u32[]{:S(2)}, u32[]{:S(2)}) %collective-permute-start.1) | collective-permute-done | bytes 32800 | tf_op jit(solution)/shard_map/ppermute | solution.py:22
  27.4 7.5 %collective-permute-start.9 = (f32[1,8,128]{2,1,0:T(8,128)S(1)}, f32[1,8,128]{2,1,0:T(8,128)S(1)}, u32[]{:S(2)}, u32[]{:S(2)}) collective-permute-start(f32[1,8,128]{2,1,0:T(8,128)S(1)} %get-tuple-element.113), channel_id=1, source_target_pairs={{0,16},{16,32},{32,48},{48,64},{64,80},{80,96},{96,112},{112,128},... | collective-permute-start | bytes 12296 | tf_op jit(solution)/shard_map/ppermute | solution.py:21
  42.8 5.8 %fusion.6 = f32[4,8,8,17,16]{4,2,3,1,0:T(8,128)} fusion(bf16[16,16,3,3,3]{1,0,4,3,2:T(8,128)(2,1)S(1)} %copy-done.23, bf16[16,6,10,1,7,2]{0,4,5,2,1,3:T(8,128)(2,1)S(1)} %slice.441, bf16[16,6,10,1,8,17]{0,4,5,2,1,3:T(8,128)(2,1)} %copy.46), kind=kOutput, calls=%fused_computation.8 | convolution fusion | flops 61037568 | bytes 580352 | tf_op jit(solution)/shard_map/conv_general_dilated | solution.py:65
  61.2 4.9 collective-permute-start.11
  66.2 4.4 collective-permute-start.6
  72.9 4.4 collective-permute-done.7
  85.1 5.8 %fusion.10 = f32[4,8,8,17,16]{4,2,3,1,0:T(8,128)} fusion(bf16[16,16,3,3,3]{1,0,4,3,2:T(8,128)(2,1)S(1)} %copy-done, bf16[16,6,10,1,7,2]{0,4,5,2,1,3:T(8,128)(2,1)S(1)} %slice.445, bf16[16,6,10,1,8,17]{0,4,5,2,1,3:T(8,128)(2,1)} %copy.50), kind=kOutput, calls=%fused_computation.11 | convolution fusion | flops 61037568 | bytes 580352 | tf_op jit(solution)/shard_map/conv_general_dilated | solution.py:65
  98.0 5.6 %collective-permute-start.12 = (f32[1,8,128]{2,1,0:T(8,128)S(1)}, f32[1,8,128]{2,1,0:T(8,128)S(1)}, u32[]{:S(2)}, u32[]{:S(2)}) collective-permute-start(f32[1,8,128]{2,1,0:T(8,128)S(1)} %get-tuple-element.112), channel_id=1, source_target_pairs={{16,0},{32,16},{48,32},{64,48},{80,64},{96,80},{112,96},{128,112},... | collective-permute-start | bytes 12296 | tf_op jit(solution)/shard_map/ppermute | solution.py:22
  110.5 5.5 %collective-permute-start.15 = (f32[6,1,128]{2,1,0:T(1,128)S(1)}, f32[6,1,128]{2,1,0:T(1,128)S(1)}, u32[]{:S(2)}, u32[]{:S(2)}) collective-permute-start(f32[6,1,128]{2,1,0:T(1,128)S(1)} %get-tuple-element.96), channel_id=1, source_target_pairs={{0,1},{1,2},{2,3},{3,4},{4,5},{5,6},{6,7},{7,8},{8,9},{9,10},{10,1... | collective-permute-start | bytes 9224 | tf_op jit(solution)/shard_map/ppermute | solution.py:21
  116.9 8.6 %collective-permute-start.16 = (f32[1,8,128]{2,1,0:T(8,128)S(1)}, f32[1,8,128]{2,1,0:T(8,128)S(1)}, u32[]{:S(2)}, u32[]{:S(2)}) collective-permute-start(f32[1,8,128]{2,1,0:T(8,128)S(1)} %get-tuple-element.110), channel_id=1, source_target_pairs={{16,0},{32,16},{48,32},{64,48},{80,64},{96,80},{112,96},{128,112},... | collective-permute-start | bytes 12296 | tf_op jit(solution)/shard_map/ppermute | solution.py:22
  130.7 6.0 %collective-permute-start.19 = (f32[6,1,128]{2,1,0:T(1,128)S(1)}, f32[6,1,128]{2,1,0:T(1,128)S(1)}, u32[]{:S(2)}, u32[]{:S(2)}) collective-permute-start(f32[6,1,128]{2,1,0:T(1,128)S(1)} %get-tuple-element.94), channel_id=1, source_target_pairs={{0,1},{1,2},{2,3},{3,4},{4,5},{5,6},{6,7},{7,8},{8,9},{9,10},{10,1... | collective-permute-start | bytes 9224 | tf_op jit(solution)/shard_map/ppermute | solution.py:21
  137.7 9.2 %collective-permute-start.20 = (f32[1,8,128]{2,1,0:T(8,128)S(1)}, f32[1,8,128]{2,1,0:T(8,128)S(1)}, u32[]{:S(2)}, u32[]{:S(2)}) collective-permute-start(f32[1,8,128]{2,1,0:T(8,128)S(1)} %get-tuple-element.108), channel_id=1, source_target_pairs={{16,0},{32,16},{48,32},{64,48},{80,64},{96,80},{112,96},{128,112},... | collective-permute-start | bytes 12296 | tf_op jit(solution)/shard_map/ppermute | solution.py:22
  151.9 6.0 %collective-permute-start.23 = (f32[6,1,128]{2,1,0:T(1,128)S(1)}, f32[6,1,128]{2,1,0:T(1,128)S(1)}, u32[]{:S(2)}, u32[]{:S(2)}) collective-permute-start(f32[6,1,128]{2,1,0:T(1,128)S(1)} %get-tuple-element.92), channel_id=1, source_target_pairs={{0,1},{1,2},{2,3},{3,4},{4,5},{5,6},{6,7},{7,8},{8,9},{9,10},{10,1... | collective-permute-start | bytes 9224 | tf_op jit(solution)/shard_map/ppermute | solution.py:21
  159.8 8.5 %collective-permute-start.24 = (bf16[1,10,128]{2,1,0:T(8,128)(2,1)S(1)}, bf16[1,10,128]{2,1,0:T(8,128)(2,1)S(1)}, u32[]{:S(2)}, u32[]{:S(2)}) collective-permute-start(bf16[1,10,128]{2,1,0:T(8,128)(2,1)S(1)} %get-tuple-element.85), channel_id=1, source_target_pairs={{0,16},{16,32},{32,48},{48,64},{64,80},{80,96},{96,112},{112,128},... | collective-permute-start | bytes 7688 | tf_op jit(solution)/shard_map/ppermute | solution.py:34
  171.2 6.0 %collective-permute-done.25 = bf16[1,10,128]{2,1,0:T(8,128)(2,1)S(1)} collective-permute-done((bf16[1,10,128]{2,1,0:T(8,128)(2,1)S(1)}, bf16[1,10,128]{2,1,0:T(8,128)(2,1)S(1)}, u32[]{:S(2)}, u32[]{:S(2)}) %collective-permute-start.25) | collective-permute-done | bytes 2592 | tf_op jit(solution)/shard_map/ppermute | solution.py:34
  177.3 6.0 %collective-permute-start.26 = (bf16[4,1,128]{2,1,0:T(2,128)(2,1)S(1)}, bf16[4,1,128]{2,1,0:T(2,128)(2,1)S(1)}, u32[]{:S(2)}, u32[]{:S(2)}) collective-permute-start(bf16[4,1,128]{2,1,0:T(2,128)(2,1)S(1)} %get-tuple-element.104), channel_id=1, source_target_pairs={{0,1},{1,2},{2,3},{3,4},{4,5},{5,6},{6,7},{7,8},{8,9},{9,10},{10,1... | collective-permute-start | bytes 3080 | tf_op jit(solution)/shard_map/ppermute | solution.py:34
  185.3 4.5 collective-permute-done.27
  197.7 5.4 %collective-permute-done.29 = bf16[1,10,128]{2,1,0:T(8,128)(2,1)S(1)} collective-permute-done((bf16[1,10,128]{2,1,0:T(8,128)(2,1)S(1)}, bf16[1,10,128]{2,1,0:T(8,128)(2,1)S(1)}, u32[]{:S(2)}, u32[]{:S(2)}) %collective-permute-start.29) | collective-permute-done | bytes 2592 | tf_op jit(solution)/shard_map/ppermute | solution.py:34
  215.1 4.6 collective-permute-start.33
  230.8 6.7 %copy.62 = bf16[16,1,6,10,130]{0,1,4,3,2:T(2,128)(2,1)} copy(bf16[16,1,6,10,130]{4,0,3,2,1:T(8,128)(2,1)S(1)} %copy-done.4) | data formatting | bytes 499200 | tf_op jit(solution)/shard_map/broadcast_in_dim | solution.py:82
  237.6 6.7 %copy.64 = bf16[16,1,6,10,130]{0,1,4,3,2:T(2,128)(2,1)} copy(bf16[16,1,6,10,130]{4,0,3,2,1:T(8,128)(2,1)S(1)} %copy-done.5) | data formatting | bytes 499200 | tf_op jit(solution)/shard_map/broadcast_in_dim | solution.py:82
  257.6 8.0 %convolution_select_fusion.1 = f32[6,10,8,17,16]{4,2,3,1,0:T(8,128)} fusion(bf16[16,16,3,3,3]{1,0,4,3,2:T(8,128)(2,1)S(1)} %copy-done, pred[8,17]{0,1:T(8,128)(4,1)S(1)} %copy-done.25, bf16[16,4,8,1,7,2]{0,4,5,2,1,3:T(8,128)(2,1)S(1)} %slice.482, bf16[16,4,8,1,8,17]{0,4,5,2,1,3:T(8,128)(2,1)} %copy.56), kind=kOutput, calls=%fused_computation.19 | convolution fusion | flops 60759552 | bytes 689800 | tf_op jit(solution)/shard_map/conv_general_dilated | solution.py:93
  265.5 6.2 %copy.57 = f32[6,10,8,17,16]{3,2,4,1,0:T(8,128)} copy(f32[6,10,8,17,16]{4,2,3,1,0:T(8,128)} %convolution_select_fusion.1) | data formatting | bytes 1044480 | tf_op jit(solution)/shard_map/conv_general_dilated | solution.py:93
  277.6 5.9 %collective-permute-start.37 = (bf16[16,1,10,128]{3,0,2,1:T(8,128)(2,1)S(1)}, bf16[16,1,10,128]{3,0,2,1:T(8,128)(2,1)S(1)}, u32[]{:S(2)}, u32[]{:S(2)}) collective-permute-start(bf16[16,1,10,128]{3,0,2,1:T(8,128)(2,1)S(1)} %get-tuple-element.52), channel_id=1, source_target_pairs={{16,0},{32,16},{48,32},{64,48},{80,64},{96,80},{112,96},{128,112},... | collective-permute-start | bytes 122888 | tf_op jit(solution)/shard_map/ppermute | solution.py:34
  283.6 29.5 %fusion.120 = f32[16,16,3,3,3]{0,1,4,3,2:T(8,128)S(1)} fusion(bf16[16,1,6,10,130]{0,1,4,3,2:T(2,128)(2,1)} %copy.64, bf16[16,1,4,8,128]{0,1,4,3,2:T(2,128)(2,1)} %copy.65), kind=kOutput, calls=%fused_computation.275 | convolution fusion | flops 56623104 | bytes 408320 | tf_op jit(solution)/shard_map/transpose | solution.py:89
  326.7 6.7 %convolution_select_fusion = f32[6,10,8,17,16]{4,2,3,1,0:T(8,128)} fusion(bf16[16,16,3,3,3]{1,0,4,3,2:T(8,128)(2,1)S(1)} %copy-done.24, pred[8,17]{0,1:T(8,128)(4,1)S(1)} %copy-done.25, bf16[16,4,8,1,7,2]{0,4,5,2,1,3:T(8,128)(2,1)S(1)} %slice.490, bf16[16,4,8,1,8,17]{0,4,5,2,1,3:T(8,128)(2,1)S(1)} %copy.60), kind=kOutput, calls=%fused_computation.18 | convolution fusion | flops 60759552 | bytes 689800 | tf_op jit(solution)/shard_map/conv_general_dilated | solution.py:93
  333.4 6.3 %copy.61 = f32[6,10,8,17,16]{3,2,4,1,0:T(8,128)} copy(f32[6,10,8,17,16]{4,2,3,1,0:T(8,128)} %convolution_select_fusion) | data formatting | bytes 1044480 | tf_op jit(solution)/shard_map/conv_general_dilated | solution.py:93
  345.7 29.8 %fusion.119 = f32[16,16,3,3,3]{0,1,4,3,2:T(8,128)} fusion(bf16[16,1,6,10,130]{0,1,4,3,2:T(2,128)(2,1)} %copy.62, bf16[16,1,4,8,128]{0,1,4,3,2:T(2,128)(2,1)S(1)} %copy.63), kind=kOutput, calls=%fused_computation.274 | convolution fusion | flops 56623104 | bytes 408320 | tf_op jit(solution)/shard_map/transpose | solution.py:89
  375.5 111.1 %all-reduce.47 = (f32[16,16,3,3,3]{0,1,4,3,2:T(8,128)S(1)}, f32[16,16,3,3,3]{0,1,4,3,2:T(8,128)S(1)}, f32[16]{0:T(128)S(1)}) all-reduce(f32[16,16,3,3,3]{0,1,4,3,2:T(8,128)} %fusion.119, f32[16,16,3,3,3]{0,1,4,3,2:T(8,128)S(1)} %fusion.120, f32[16]{0:T(128)S(1)} %convolution_bitcast_fusion), channel_id=1, replica_groups=mesh['gz'=32,'gy'=16] {'gz','gy'}, use_global_device_ids=true, to_apply=%region_0.1 | all-reduce | flops 13840 | bytes 110720 | tf_op jit(solution)/shard_map/psum | solution.py:164
  495.4 6.9 %collective-permute-done.41 = bf16[16,1,10,128]{3,0,2,1:T(8,128)(2,1)S(1)} collective-permute-done((bf16[16,1,10,128]{3,0,2,1:T(8,128)(2,1)S(1)}, bf16[16,1,10,128]{3,0,2,1:T(8,128)(2,1)S(1)}, u32[]{:S(2)}, u32[]{:S(2)}) %collective-permute-start.41) | collective-permute-done | bytes 40992 | tf_op jit(solution)/shard_map/ppermute | solution.py:34
  502.5 5.4 %collective-permute-start.42 = (bf16[16,4,1,128]{3,0,2,1:T(8,128)(2,1)S(1)}, bf16[16,4,1,128]{3,0,2,1:T(8,128)(2,1)S(1)}, u32[]{:S(2)}, u32[]{:S(2)}) collective-permute-start(bf16[16,4,1,128]{3,0,2,1:T(8,128)(2,1)S(1)} %get-tuple-element.61), channel_id=1, source_target_pairs={{0,1},{1,2},{2,3},{3,4},{4,5},{5,6},{6,7},{7,8},{8,9},{9,10},{10,1... | collective-permute-start | bytes 49160 | tf_op jit(solution)/shard_map/ppermute | solution.py:34
  (226 shorter events, 158.6 us)
Async XLA Ops:
  1.5 12.1 %collective-permute-start = (bf16[16,1,8,128]{3,0,2,1:T(8,128)(2,1)S(1)}, bf16[16,1,8,128]{3,0,2,1:T(8,128)(2,1)S(1)}, u32[]{:S(2)}, u32[]{:S(2)}) collective-permute-start(bf16[16,1,8,128]{3,0,2,1:T(8,128)(2,1)S(1)} %copy.83), channel_id=1, source_target_pairs={{0,16},{16,32},{32,48},{48,64},{64,80},{80,96},{96,112},{112,128},... | collective-permute-start | bytes 98312 | tf_op jit(solution)/shard_map/ppermute | solution.py:21
  10.9 9.1 %collective-permute-start.1 = (bf16[16,1,8,128]{3,0,2,1:T(8,128)(2,1)S(1)}, bf16[16,1,8,128]{3,0,2,1:T(8,128)(2,1)S(1)}, u32[]{:S(2)}, u32[]{:S(2)}) collective-permute-start(bf16[16,1,8,128]{3,0,2,1:T(8,128)(2,1)S(1)} %copy.84), channel_id=1, source_target_pairs={{16,0},{32,16},{48,32},{64,48},{80,64},{96,80},{112,96},{128,112},... | collective-permute-start | bytes 98312 | tf_op jit(solution)/shard_map/ppermute | solution.py:22
  20.0 14.9 %collective-permute-start.2 = (bf16[16,6,1,128]{3,0,2,1:T(8,128)(2,1)S(1)}, bf16[16,6,1,128]{3,0,2,1:T(8,128)(2,1)S(1)}, u32[]{:S(2)}, u32[]{:S(2)}) collective-permute-start(bf16[16,6,1,128]{3,0,2,1:T(8,128)(2,1)S(1)} %get-tuple-element.59), channel_id=1, source_target_pairs={{0,1},{1,2},{2,3},{3,4},{4,5},{5,6},{6,7},{7,8},{8,9},{9,10},{10,1... | collective-permute-start | bytes 73736 | tf_op jit(solution)/shard_map/ppermute | solution.py:21
  23.5 11.4 %collective-permute-start.3 = (bf16[16,6,1,128]{3,0,2,1:T(8,128)(2,1)S(1)}, bf16[16,6,1,128]{3,0,2,1:T(8,128)(2,1)S(1)}, u32[]{:S(2)}, u32[]{:S(2)}) collective-permute-start(bf16[16,6,1,128]{3,0,2,1:T(8,128)(2,1)S(1)} %get-tuple-element.60), channel_id=1, source_target_pairs={{1,0},{2,1},{3,2},{4,3},{5,4},{6,5},{7,6},{8,7},{9,8},{10,9},{11,1... | collective-permute-start | bytes 73736 | tf_op jit(solution)/shard_map/ppermute | solution.py:22
  25.4 33.2 %collective-permute-start.8 = (f32[1,8,128]{2,1,0:T(8,128)S(1)}, f32[1,8,128]{2,1,0:T(8,128)S(1)}, u32[]{:S(2)}, u32[]{:S(2)}) collective-permute-start(f32[1,8,128]{2,1,0:T(8,128)S(1)} %get-tuple-element.114), channel_id=1, source_target_pairs={{16,0},{32,16},{48,32},{64,48},{80,64},{96,80},{112,96},{128,112},... | collective-permute-start | bytes 12296 | tf_op jit(solution)/shard_map/ppermute | solution.py:22
  27.4 31.3 %collective-permute-start.9 = (f32[1,8,128]{2,1,0:T(8,128)S(1)}, f32[1,8,128]{2,1,0:T(8,128)S(1)}, u32[]{:S(2)}, u32[]{:S(2)}) collective-permute-start(f32[1,8,128]{2,1,0:T(8,128)S(1)} %get-tuple-element.113), channel_id=1, source_target_pairs={{0,16},{16,32},{32,48},{48,64},{64,80},{80,96},{96,112},{112,128},... | collective-permute-start | bytes 12296 | tf_op jit(solution)/shard_map/ppermute | solution.py:21
  53.3 12.9 %collective-permute-start.4 = (bf16[16,1,8,128]{3,0,2,1:T(8,128)(2,1)S(1)}, bf16[16,1,8,128]{3,0,2,1:T(8,128)(2,1)S(1)}, u32[]{:S(2)}, u32[]{:S(2)}) collective-permute-start(bf16[16,1,8,128]{3,0,2,1:T(8,128)(2,1)S(1)} %get-tuple-element.65), channel_id=1, source_target_pairs={{0,16},{16,32},{32,48},{48,64},{64,80},{80,96},{96,112},{112,128},... | collective-permute-start | bytes 98312 | tf_op jit(solution)/shard_map/ppermute | solution.py:21
  56.7 9.4 %collective-permute-start.5 = (bf16[16,1,8,128]{3,0,2,1:T(8,128)(2,1)S(1)}, bf16[16,1,8,128]{3,0,2,1:T(8,128)(2,1)S(1)}, u32[]{:S(2)}, u32[]{:S(2)}) collective-permute-start(bf16[16,1,8,128]{3,0,2,1:T(8,128)(2,1)S(1)} %get-tuple-element.66), channel_id=1, source_target_pairs={{16,0},{32,16},{48,32},{64,48},{80,64},{96,80},{112,96},{128,112},... | collective-permute-start | bytes 98312 | tf_op jit(solution)/shard_map/ppermute | solution.py:22
  58.7 14.0 %collective-permute-start.10 = (f32[6,1,128]{2,1,0:T(1,128)S(1)}, f32[6,1,128]{2,1,0:T(1,128)S(1)}, u32[]{:S(2)}, u32[]{:S(2)}) collective-permute-start(f32[6,1,128]{2,1,0:T(1,128)S(1)} %get-tuple-element.99), channel_id=1, source_target_pairs={{1,0},{2,1},{3,2},{4,3},{5,4},{6,5},{7,6},{8,7},{9,8},{10,9},{11,1... | collective-permute-start | bytes 9224 | tf_op jit(solution)/shard_map/ppermute | solution.py:22
  61.2 11.5 %collective-permute-start.11 = (f32[6,1,128]{2,1,0:T(1,128)S(1)}, f32[6,1,128]{2,1,0:T(1,128)S(1)}, u32[]{:S(2)}, u32[]{:S(2)}) collective-permute-start(f32[6,1,128]{2,1,0:T(1,128)S(1)} %get-tuple-element.98), channel_id=1, source_target_pairs={{0,1},{1,2},{2,3},{3,4},{4,5},{5,6},{6,7},{7,8},{8,9},{9,10},{10,1... | collective-permute-start | bytes 9224 | tf_op jit(solution)/shard_map/ppermute | solution.py:21
  98.0 9.8 %collective-permute-start.12 = (f32[1,8,128]{2,1,0:T(8,128)S(1)}, f32[1,8,128]{2,1,0:T(8,128)S(1)}, u32[]{:S(2)}, u32[]{:S(2)}) collective-permute-start(f32[1,8,128]{2,1,0:T(8,128)S(1)} %get-tuple-element.112), channel_id=1, source_target_pairs={{16,0},{32,16},{48,32},{64,48},{80,64},{96,80},{112,96},{128,112},... | collective-permute-start | bytes 12296 | tf_op jit(solution)/shard_map/ppermute | solution.py:22
  108.5 7.4 %collective-permute-start.14 = (f32[6,1,128]{2,1,0:T(1,128)S(1)}, f32[6,1,128]{2,1,0:T(1,128)S(1)}, u32[]{:S(2)}, u32[]{:S(2)}) collective-permute-start(f32[6,1,128]{2,1,0:T(1,128)S(1)} %get-tuple-element.97), channel_id=1, source_target_pairs={{1,0},{2,1},{3,2},{4,3},{5,4},{6,5},{7,6},{8,7},{9,8},{10,9},{11,1... | collective-permute-start | bytes 9224 | tf_op jit(solution)/shard_map/ppermute | solution.py:22
  116.9 11.2 %collective-permute-start.16 = (f32[1,8,128]{2,1,0:T(8,128)S(1)}, f32[1,8,128]{2,1,0:T(8,128)S(1)}, u32[]{:S(2)}, u32[]{:S(2)}) collective-permute-start(f32[1,8,128]{2,1,0:T(8,128)S(1)} %get-tuple-element.110), channel_id=1, source_target_pairs={{16,0},{32,16},{48,32},{64,48},{80,64},{96,80},{112,96},{128,112},... | collective-permute-start | bytes 12296 | tf_op jit(solution)/shard_map/ppermute | solution.py:22
  128.8 7.9 %collective-permute-start.18 = (f32[6,1,128]{2,1,0:T(1,128)S(1)}, f32[6,1,128]{2,1,0:T(1,128)S(1)}, u32[]{:S(2)}, u32[]{:S(2)}) collective-permute-start(f32[6,1,128]{2,1,0:T(1,128)S(1)} %get-tuple-element.95), channel_id=1, source_target_pairs={{1,0},{2,1},{3,2},{4,3},{5,4},{6,5},{7,6},{8,7},{9,8},{10,9},{11,1... | collective-permute-start | bytes 9224 | tf_op jit(solution)/shard_map/ppermute | solution.py:22
  130.7 6.7 %collective-permute-start.19 = (f32[6,1,128]{2,1,0:T(1,128)S(1)}, f32[6,1,128]{2,1,0:T(1,128)S(1)}, u32[]{:S(2)}, u32[]{:S(2)}) collective-permute-start(f32[6,1,128]{2,1,0:T(1,128)S(1)} %get-tuple-element.94), channel_id=1, source_target_pairs={{0,1},{1,2},{2,3},{3,4},{4,5},{5,6},{6,7},{7,8},{8,9},{9,10},{10,1... | collective-permute-start | bytes 9224 | tf_op jit(solution)/shard_map/ppermute | solution.py:21
  137.7 11.1 %collective-permute-start.20 = (f32[1,8,128]{2,1,0:T(8,128)S(1)}, f32[1,8,128]{2,1,0:T(8,128)S(1)}, u32[]{:S(2)}, u32[]{:S(2)}) collective-permute-start(f32[1,8,128]{2,1,0:T(8,128)S(1)} %get-tuple-element.108), channel_id=1, source_target_pairs={{16,0},{32,16},{48,32},{64,48},{80,64},{96,80},{112,96},{128,112},... | collective-permute-start | bytes 12296 | tf_op jit(solution)/shard_map/ppermute | solution.py:22
  150.0 7.9 %collective-permute-start.22 = (f32[6,1,128]{2,1,0:T(1,128)S(1)}, f32[6,1,128]{2,1,0:T(1,128)S(1)}, u32[]{:S(2)}, u32[]{:S(2)}) collective-permute-start(f32[6,1,128]{2,1,0:T(1,128)S(1)} %get-tuple-element.93), channel_id=1, source_target_pairs={{1,0},{2,1},{3,2},{4,3},{5,4},{6,5},{7,6},{8,7},{9,8},{10,9},{11,1... | collective-permute-start | bytes 9224 | tf_op jit(solution)/shard_map/ppermute | solution.py:22
  151.9 6.7 %collective-permute-start.23 = (f32[6,1,128]{2,1,0:T(1,128)S(1)}, f32[6,1,128]{2,1,0:T(1,128)S(1)}, u32[]{:S(2)}, u32[]{:S(2)}) collective-permute-start(f32[6,1,128]{2,1,0:T(1,128)S(1)} %get-tuple-element.92), channel_id=1, source_target_pairs={{0,1},{1,2},{2,3},{3,4},{4,5},{5,6},{6,7},{7,8},{8,9},{9,10},{10,1... | collective-permute-start | bytes 9224 | tf_op jit(solution)/shard_map/ppermute | solution.py:21
  159.8 11.4 %collective-permute-start.24 = (bf16[1,10,128]{2,1,0:T(8,128)(2,1)S(1)}, bf16[1,10,128]{2,1,0:T(8,128)(2,1)S(1)}, u32[]{:S(2)}, u32[]{:S(2)}) collective-permute-start(bf16[1,10,128]{2,1,0:T(8,128)(2,1)S(1)} %get-tuple-element.85), channel_id=1, source_target_pairs={{0,16},{16,32},{32,48},{48,64},{64,80},{80,96},{96,112},{112,128},... | collective-permute-start | bytes 7688 | tf_op jit(solution)/shard_map/ppermute | solution.py:34
  168.4 8.8 %collective-permute-start.25 = (bf16[1,10,128]{2,1,0:T(8,128)(2,1)S(1)}, bf16[1,10,128]{2,1,0:T(8,128)(2,1)S(1)}, u32[]{:S(2)}, u32[]{:S(2)}) collective-permute-start(bf16[1,10,128]{2,1,0:T(8,128)(2,1)S(1)} %get-tuple-element.86), channel_id=1, source_target_pairs={{16,0},{32,16},{48,32},{64,48},{80,64},{96,80},{112,96},{128,112},... | collective-permute-start | bytes 7688 | tf_op jit(solution)/shard_map/ppermute | solution.py:34
  177.3 8.0 %collective-permute-start.26 = (bf16[4,1,128]{2,1,0:T(2,128)(2,1)S(1)}, bf16[4,1,128]{2,1,0:T(2,128)(2,1)S(1)}, u32[]{:S(2)}, u32[]{:S(2)}) collective-permute-start(bf16[4,1,128]{2,1,0:T(2,128)(2,1)S(1)} %get-tuple-element.104), channel_id=1, source_target_pairs={{0,1},{1,2},{2,3},{3,4},{4,5},{5,6},{6,7},{7,8},{8,9},{9,10},{10,1... | collective-permute-start | bytes 3080 | tf_op jit(solution)/shard_map/ppermute | solution.py:34
  190.5 7.1 %collective-permute-start.28 = (bf16[1,10,128]{2,1,0:T(8,128)(2,1)S(1)}, bf16[1,10,128]{2,1,0:T(8,128)(2,1)S(1)}, u32[]{:S(2)}, u32[]{:S(2)}) collective-permute-start(bf16[1,10,128]{2,1,0:T(8,128)(2,1)S(1)} %get-tuple-element.83), channel_id=1, source_target_pairs={{0,16},{16,32},{32,48},{48,64},{64,80},{80,96},{96,112},{112,128},... | collective-permute-start | bytes 7688 | tf_op jit(solution)/shard_map/ppermute | solution.py:34
  193.9 9.1 %collective-permute-start.29 = (bf16[1,10,128]{2,1,0:T(8,128)(2,1)S(1)}, bf16[1,10,128]{2,1,0:T(8,128)(2,1)S(1)}, u32[]{:S(2)}, u32[]{:S(2)}) collective-permute-start(bf16[1,10,128]{2,1,0:T(8,128)(2,1)S(1)} %get-tuple-element.84), channel_id=1, source_target_pairs={{16,0},{32,16},{48,32},{64,48},{80,64},{96,80},{112,96},{128,112},... | collective-permute-start | bytes 7688 | tf_op jit(solution)/shard_map/ppermute | solution.py:34
  212.3 7.4 %collective-permute-start.32 = (bf16[1,10,128]{2,1,0:T(8,128)(2,1)S(1)}, bf16[1,10,128]{2,1,0:T(8,128)(2,1)S(1)}, u32[]{:S(2)}, u32[]{:S(2)}) collective-permute-start(bf16[1,10,128]{2,1,0:T(8,128)(2,1)S(1)} %get-tuple-element.81), channel_id=1, source_target_pairs={{0,16},{16,32},{32,48},{48,64},{64,80},{80,96},{96,112},{112,128},... | collective-permute-start | bytes 7688 | tf_op jit(solution)/shard_map/ppermute | solution.py:34
  215.1 8.8 %collective-permute-start.33 = (bf16[1,10,128]{2,1,0:T(8,128)(2,1)S(1)}, bf16[1,10,128]{2,1,0:T(8,128)(2,1)S(1)}, u32[]{:S(2)}, u32[]{:S(2)}) collective-permute-start(bf16[1,10,128]{2,1,0:T(8,128)(2,1)S(1)} %get-tuple-element.82), channel_id=1, source_target_pairs={{16,0},{32,16},{48,32},{64,48},{80,64},{96,80},{112,96},{128,112},... | collective-permute-start | bytes 7688 | tf_op jit(solution)/shard_map/ppermute | solution.py:34
  225.3 22.1 %collective-permute-start.34 = (bf16[4,1,128]{2,1,0:T(2,128)(2,1)}, bf16[4,1,128]{2,1,0:T(2,128)(2,1)}, u32[]{:S(2)}, u32[]{:S(2)}) collective-permute-start(bf16[4,1,128]{2,1,0:T(2,128)(2,1)} %get-tuple-element.100), channel_id=1, source_target_pairs={{0,1},{1,2},{2,3},{3,4},{4,5},{5,6},{6,7},{7,8},{8,9},{9,10},{10,1... | collective-permute-start | bytes 3080 | tf_op jit(solution)/shard_map/ppermute | solution.py:34
  227.2 20.1 %collective-permute-start.35 = (bf16[4,1,128]{2,1,0:T(2,128)(2,1)}, bf16[4,1,128]{2,1,0:T(2,128)(2,1)}, u32[]{:S(2)}, u32[]{:S(2)}) collective-permute-start(bf16[4,1,128]{2,1,0:T(2,128)(2,1)} %get-tuple-element.101), channel_id=1, source_target_pairs={{1,0},{2,1},{3,2},{4,3},{5,4},{6,5},{7,6},{8,7},{9,8},{10,9},{11,1... | collective-permute-start | bytes 3080 | tf_op jit(solution)/shard_map/ppermute | solution.py:34
  275.1 38.1 %collective-permute-start.36 = (bf16[16,1,10,128]{3,0,2,1:T(8,128)(2,1)S(1)}, bf16[16,1,10,128]{3,0,2,1:T(8,128)(2,1)S(1)}, u32[]{:S(2)}, u32[]{:S(2)}) collective-permute-start(bf16[16,1,10,128]{3,0,2,1:T(8,128)(2,1)S(1)} %get-tuple-element.51), channel_id=1, source_target_pairs={{0,16},{16,32},{32,48},{48,64},{64,80},{80,96},{96,112},{112,128},... | collective-permute-start | bytes 122888 | tf_op jit(solution)/shard_map/ppermute | solution.py:34
  277.6 35.6 %collective-permute-start.37 = (bf16[16,1,10,128]{3,0,2,1:T(8,128)(2,1)S(1)}, bf16[16,1,10,128]{3,0,2,1:T(8,128)(2,1)S(1)}, u32[]{:S(2)}, u32[]{:S(2)}) collective-permute-start(bf16[16,1,10,128]{3,0,2,1:T(8,128)(2,1)S(1)} %get-tuple-element.52), channel_id=1, source_target_pairs={{16,0},{32,16},{48,32},{64,48},{80,64},{96,80},{112,96},{128,112},... | collective-permute-start | bytes 122888 | tf_op jit(solution)/shard_map/ppermute | solution.py:34
  492.9 9.4 %collective-permute-start.41 = (bf16[16,1,10,128]{3,0,2,1:T(8,128)(2,1)S(1)}, bf16[16,1,10,128]{3,0,2,1:T(8,128)(2,1)S(1)}, u32[]{:S(2)}, u32[]{:S(2)}) collective-permute-start(bf16[16,1,10,128]{3,0,2,1:T(8,128)(2,1)S(1)} %get-tuple-element.50), channel_id=1, source_target_pairs={{16,0},{32,16},{48,32},{64,48},{80,64},{96,80},{112,96},{128,112},... | collective-permute-start | bytes 122888 | tf_op jit(solution)/shard_map/ppermute | solution.py:34
  502.5 9.5 %collective-permute-start.42 = (bf16[16,4,1,128]{3,0,2,1:T(8,128)(2,1)S(1)}, bf16[16,4,1,128]{3,0,2,1:T(8,128)(2,1)S(1)}, u32[]{:S(2)}, u32[]{:S(2)}) collective-permute-start(bf16[16,4,1,128]{3,0,2,1:T(8,128)(2,1)S(1)} %get-tuple-element.61), channel_id=1, source_target_pairs={{0,1},{1,2},{2,3},{3,4},{4,5},{5,6},{6,7},{7,8},{8,9},{9,10},{10,1... | collective-permute-start | bytes 49160 | tf_op jit(solution)/shard_map/ppermute | solution.py:34
  507.9 6.9 %collective-permute-start.43 = (bf16[16,4,1,128]{3,0,2,1:T(8,128)(2,1)S(1)}, bf16[16,4,1,128]{3,0,2,1:T(8,128)(2,1)S(1)}, u32[]{:S(2)}, u32[]{:S(2)}) collective-permute-start(bf16[16,4,1,128]{3,0,2,1:T(8,128)(2,1)S(1)} %get-tuple-element.62), channel_id=1, source_target_pairs={{1,0},{2,1},{3,2},{4,3},{5,4},{6,5},{7,6},{8,7},{9,8},{10,9},{11,1... | collective-permute-start | bytes 49160 | tf_op jit(solution)/shard_map/ppermute | solution.py:34
  (38 other events, 1008.6 us)
where the time goes:
time: 524 us; the launch traced here: 516 us
  starting transfers between devices  171 us (33%)
  blocking collectives  111 us (21%)
  matrix products  86.3 us (16%)
  local copies, waits for them, and re-layouts  78.4 us (15%)
  waiting for transfers between devices  51.9 us (10%)
  other arithmetic  12.8 us (2%)
    psum x1, blocking collectives, on_device(): lax.psum((raw_first, raw_second, raw_speed), ('gz', 'gy'))  111 us
    ppermute x20, starting transfers between devices, from_behind(): return lax.ppermute(block, axis, route)  70.3 us
    ppermute x12, starting transfers between devices, extended(): before = lax.ppermute(last, axis, up)  59.5 us
    transpose x2, matrix products, weight_grad(): return d_weight.transpose(1, 0, 2, 3, 4)  59.3 us
    ppermute x12, starting transfers between devices, extended(): after = lax.ppermute(initial, axis, down)  41.2 us
    ppermute x20, waiting for transfers between devices, from_behind(): return lax.ppermute(block, axis, route)  37.2 us
    conv_general_dilated x10, local copies, waits for them, and re-layouts, conv_back(): lax.conv_general_dilated(d_out[None], flip_weight(weight), (1, 1, 1), ((2...  25.9 us
    conv_general_dilated x12, local copies, waits for them, and re-layouts, conv_local(): lax.conv_general_dilated(grid[None], weight, (1, 1, 1), 'VALID', dimensio...  22 us
  transfers between devices with their start and end apart: 44, of which 16 were waited for; matrix products, arithmetic and copies ran while one was open for 13% of the time, Pallas kernels for 0%

commit v1 on v0

--- a/solution.py
+++ b/solution.py
@@ -2,6 +2,7 @@
 import jax.numpy as jnp
 from jax import lax
 from jax.sharding import PartitionSpec as P
+from jax.lax import psum
 
 C = 16
 STEPS = 4
@@ -9,6 +10,9 @@
 spread_rate = 0.5
 slope_floor = 0.1
 layout = ("NCDHW", "OIDHW", "NCDHW")
+assign_grid = lambda mine, axis_tag, row_axis: psum(
+    psum(mine, axis_name=axis_tag), axis_name=row_axis
+)
 
 
 def extended(value, sides, width):
@@ -161,7 +165,7 @@
     d_first = (d_hidden * silu_slope(act_first)).astype(jnp.bfloat16)
     raw_first = weight_grad(feat_pad, d_first)
     d_feat = input_grad(conv_first, d_first)
-    raw_first, raw_second, raw_speed = lax.psum((raw_first, raw_second, raw_speed), ("gz", "gy"))
+    raw_first, raw_second, raw_speed = assign_grid((raw_first, raw_second, raw_speed), "gz", "gy")
     total = (
         jnp.sum(raw_first * raw_first)
         + jnp.sum(raw_second * raw_second)

time: 524 us -> 654 us (1.25)
  the two profiles are of different devices: /device:TPU:15 before, /device:TPU:1 now
where the time goes in v1:
time: 654 us; the launch traced here: 646 us
  blocking collectives  235 us (36%)
  starting transfers between devices  174 us (27%)
  matrix products  86.5 us (13%)
  local copies, waits for them, and re-layouts  78.3 us (12%)
  waiting for transfers between devices  54.9 us (8%)
  other arithmetic  12.8 us (2%)
    psum x1, blocking collectives, psum(mine, axis_name=axis_tag)  169 us
    ppermute x20, starting transfers between devices, from_behind(): return lax.ppermute(block, axis, route)  81.5 us
    ppermute x12, starting transfers between devices, extended(): before = lax.ppermute(last, axis, up)  73.4 us
    psum x1, blocking collectives, psum(psum(mine, axis_name=axis_tag), axis_name=row_axis)  66 us
    transpose x2, matrix products, weight_grad(): return d_weight.transpose(1, 0, 2, 3, 4)  59.5 us
    ppermute x20, waiting for transfers between devices, from_behind(): return lax.ppermute(block, axis, route)  40.9 us
    conv_general_dilated x10, local copies, waits for them, and re-layouts, conv_back(): lax.conv_general_dilated(d_out[None], flip_weight(weight), (1, 1, 1), ((2...  25.9 us
    conv_general_dilated x12, local copies, waits for them, and re-layouts, conv_local(): lax.conv_general_dilated(grid[None], weight, (1, 1, 1), 'VALID', dimensio...  22 us
  transfers between devices with their start and end apart: 44, of which 17 were waited for; matrix products, arithmetic and copies ran while one was open for 11% of the time, Pallas kernels for 0%

profile of v1, /device:TPU:1, one launch (start us, length us, event | category | flops | bytes accessed | tf_op | source)
XLA Modules:
  0.0 646.0 jit_solution(11685186355057886530)
XLA Ops:
  1.5 10.2 %collective-permute-start = (bf16[16,1,8,128]{3,0,2,1:T(8,128)(2,1)S(1)}, bf16[16,1,8,128]{3,0,2,1:T(8,128)(2,1)S(1)}, u32[]{:S(2)}, u32[]{:S(2)}) collective-permute-start(bf16[16,1,8,128]{3,0,2,1:T(8,128)(2,1)S(1)} %copy.83), channel_id=1, source_target_pairs={{0,16},{16,32},{32,48},{48,64},{64,80},{80,96},{96,112},{112,128},... | collective-permute-start | bytes 98312 | tf_op jit(solution)/shard_map/ppermute | solution.py:25
  15.3 5.5 collective-permute-done.1
  27.2 7.5 %collective-permute-start.9 = (f32[1,8,128]{2,1,0:T(8,128)S(1)}, f32[1,8,128]{2,1,0:T(8,128)S(1)}, u32[]{:S(2)}, u32[]{:S(2)}) collective-permute-start(f32[1,8,128]{2,1,0:T(8,128)S(1)} %get-tuple-element.116), channel_id=1, source_target_pairs={{0,16},{16,32},{32,48},{48,64},{64,80},{80,96},{96,112},{112,128},... | collective-permute-start | bytes 12296 | tf_op jit(solution)/shard_map/ppermute | solution.py:25
  42.7 5.8 fusion.6
  59.9 4.6 collective-permute-start.11
  82.3 5.8 fusion.10
  97.0 7.9 %collective-permute-start.13 = (f32[1,8,128]{2,1,0:T(8,128)S(1)}, f32[1,8,128]{2,1,0:T(8,128)S(1)}, u32[]{:S(2)}, u32[]{:S(2)}) collective-permute-start(f32[1,8,128]{2,1,0:T(8,128)S(1)} %get-tuple-element.114), channel_id=1, source_target_pairs={{0,16},{16,32},{32,48},{48,64},{64,80},{80,96},{96,112},{112,128},... | collective-permute-start | bytes 12296 | tf_op jit(solution)/shard_map/ppermute | solution.py:25
  106.9 4.8 collective-permute-start.15
  114.7 8.9 %collective-permute-start.17 = (f32[1,8,128]{2,1,0:T(8,128)S(1)}, f32[1,8,128]{2,1,0:T(8,128)S(1)}, u32[]{:S(2)}, u32[]{:S(2)}) collective-permute-start(f32[1,8,128]{2,1,0:T(8,128)S(1)} %get-tuple-element.112), channel_id=1, source_target_pairs={{0,16},{16,32},{32,48},{48,64},{64,80},{80,96},{96,112},{112,128},... | collective-permute-start | bytes 12296 | tf_op jit(solution)/shard_map/ppermute | solution.py:25
  133.1 8.9 %collective-permute-start.21 = (f32[1,8,128]{2,1,0:T(8,128)S(1)}, f32[1,8,128]{2,1,0:T(8,128)S(1)}, u32[]{:S(2)}, u32[]{:S(2)}) collective-permute-start(f32[1,8,128]{2,1,0:T(8,128)S(1)} %get-tuple-element.110), channel_id=1, source_target_pairs={{0,16},{16,32},{32,48},{48,64},{64,80},{80,96},{96,112},{112,128},... | collective-permute-start | bytes 12296 | tf_op jit(solution)/shard_map/ppermute | solution.py:25
  144.1 5.2 collective-permute-start.23
  151.2 8.9 %collective-permute-start.24 = (bf16[1,10,128]{2,1,0:T(8,128)(2,1)S(1)}, bf16[1,10,128]{2,1,0:T(8,128)(2,1)S(1)}, u32[]{:S(2)}, u32[]{:S(2)}) collective-permute-start(bf16[1,10,128]{2,1,0:T(8,128)(2,1)S(1)} %get-tuple-element.88), channel_id=1, source_target_pairs={{0,16},{16,32},{32,48},{48,64},{64,80},{80,96},{96,112},{112,128},... | collective-permute-start | bytes 7688 | tf_op jit(solution)/shard_map/ppermute | solution.py:38
  162.1 6.9 %collective-permute-done.25 = bf16[1,10,128]{2,1,0:T(8,128)(2,1)S(1)} collective-permute-done((bf16[1,10,128]{2,1,0:T(8,128)(2,1)S(1)}, bf16[1,10,128]{2,1,0:T(8,128)(2,1)S(1)}, u32[]{:S(2)}, u32[]{:S(2)}) %collective-permute-start.25) | collective-permute-done | bytes 2592 | tf_op jit(solution)/shard_map/ppermute | solution.py:38
  169.1 5.7 collective-permute-start.26
  176.2 5.7 collective-permute-done.27
  187.7 6.9 %collective-permute-done.29 = bf16[1,10,128]{2,1,0:T(8,128)(2,1)S(1)} collective-permute-done((bf16[1,10,128]{2,1,0:T(8,128)(2,1)S(1)}, bf16[1,10,128]{2,1,0:T(8,128)(2,1)S(1)}, u32[]{:S(2)}, u32[]{:S(2)}) %collective-permute-start.29) | collective-permute-done | bytes 2592 | tf_op jit(solution)/shard_map/ppermute | solution.py:38
  194.7 6.0 collective-permute-start.30
  202.1 5.7 collective-permute-done.31
  213.6 6.9 %collective-permute-done.33 = bf16[1,10,128]{2,1,0:T(8,128)(2,1)S(1)} collective-permute-done((bf16[1,10,128]{2,1,0:T(8,128)(2,1)S(1)}, bf16[1,10,128]{2,1,0:T(8,128)(2,1)S(1)}, u32[]{:S(2)}, u32[]{:S(2)}) %collective-permute-start.33) | collective-permute-done | bytes 2592 | tf_op jit(solution)/shard_map/ppermute | solution.py:38
  221.7 6.3 collective-permute-start.34
  229.6 6.7 %copy.62 = bf16[16,1,6,10,130]{0,1,4,3,2:T(2,128)(2,1)} copy(bf16[16,1,6,10,130]{4,0,3,2,1:T(8,128)(2,1)S(1)} %copy-done.4) | data formatting | bytes 499200 | tf_op jit(solution)/shard_map/broadcast_in_dim | solution.py:86
  236.3 6.7 %copy.64 = bf16[16,1,6,10,130]{0,1,4,3,2:T(2,128)(2,1)} copy(bf16[16,1,6,10,130]{4,0,3,2,1:T(8,128)(2,1)S(1)} %copy-done.5) | data formatting | bytes 499200 | tf_op jit(solution)/shard_map/broadcast_in_dim | solution.py:86
  256.3 8.0 %convolution_select_fusion.1 = f32[6,10,8,17,16]{4,2,3,1,0:T(8,128)} fusion(bf16[16,16,3,3,3]{1,0,4,3,2:T(8,128)(2,1)S(1)} %copy-done, pred[8,17]{0,1:T(8,128)(4,1)S(1)} %copy-done.25, bf16[16,4,8,1,7,2]{0,4,5,2,1,3:T(8,128)(2,1)S(1)} %slice.482, bf16[16,4,8,1,8,17]{0,4,5,2,1,3:T(8,128)(2,1)} %copy.56), kind=kOutput, calls=%fused_computation.19 | convolution fusion | flops 60759552 | bytes 689800 | tf_op jit(solution)/shard_map/conv_general_dilated | solution.py:97
  264.2 6.2 copy.57
  278.6 29.5 %fusion.120 = f32[16,16,3,3,3]{0,1,4,3,2:T(8,128)S(1)} fusion(bf16[16,1,6,10,130]{0,1,4,3,2:T(2,128)(2,1)} %copy.64, bf16[16,1,4,8,128]{0,1,4,3,2:T(2,128)(2,1)} %copy.65), kind=kOutput, calls=%fused_computation.275 | convolution fusion | flops 56623104 | bytes 408320 | tf_op jit(solution)/shard_map/transpose | solution.py:93
  320.4 6.8 %convolution_select_fusion = f32[6,10,8,17,16]{4,2,3,1,0:T(8,128)} fusion(bf16[16,16,3,3,3]{1,0,4,3,2:T(8,128)(2,1)S(1)} %copy-done.24, pred[8,17]{0,1:T(8,128)(4,1)S(1)} %copy-done.25, bf16[16,4,8,1,7,2]{0,4,5,2,1,3:T(8,128)(2,1)S(1)} %slice.490, bf16[16,4,8,1,8,17]{0,4,5,2,1,3:T(8,128)(2,1)S(1)} %copy.60), kind=kOutput, calls=%fused_computation.18 | convolution fusion | flops 60759552 | bytes 689800 | tf_op jit(solution)/shard_map/conv_general_dilated | solution.py:97
  327.1 6.3 copy.61
  339.5 29.9 %fusion.119 = f32[16,16,3,3,3]{0,1,4,3,2:T(8,128)} fusion(bf16[16,1,6,10,130]{0,1,4,3,2:T(2,128)(2,1)} %copy.62, bf16[16,1,4,8,128]{0,1,4,3,2:T(2,128)(2,1)S(1)} %copy.63), kind=kOutput, calls=%fused_computation.274 | convolution fusion | flops 56623104 | bytes 408320 | tf_op jit(solution)/shard_map/transpose | solution.py:93
  369.4 169.0 %all-reduce.47 = (f32[16,16,3,3,3]{0,1,4,3,2:T(8,128)S(1)}, f32[16,16,3,3,3]{0,1,4,3,2:T(8,128)S(1)}, f32[16]{0:T(128)S(1)}) all-reduce(f32[16,16,3,3,3]{0,1,4,3,2:T(8,128)} %fusion.119, f32[16,16,3,3,3]{0,1,4,3,2:T(8,128)S(1)} %fusion.120, f32[16]{0:T(128)S(1)} %convolution_bitcast_fusion), channel_id=1, replica_groups=mesh['gz'=32,'gy'=16] {'gz'}, use_global_device_ids=true, to_apply=%region_0.1 | all-reduce | flops 13840 | bytes 110720 | tf_op jit(solution)/shard_map/psum | solution.py:14
  538.4 66.0 %all-reduce.48 = (f32[16,16,3,3,3]{0,1,4,3,2:T(8,128)S(1)}, f32[16,16,3,3,3]{0,1,4,3,2:T(8,128)S(1)}, f32[16]{0:T(128)S(1)}) all-reduce(f32[16,16,3,3,3]{0,1,4,3,2:T(8,128)S(1)} %get-tuple-element.16, f32[16,16,3,3,3]{0,1,4,3,2:T(8,128)S(1)} %get-tuple-element.17, f32[16]{0:T(128)S(1)} %get-tuple-element.18), channel_id=1, replica_groups=mesh['gz'=32,'gy'=16] {'gy'}, use_global_device_ids=true, to_apply=%region_1.2 | all-reduce | flops 13840 | bytes 110720 | tf_op jit(solution)/shard_map/psum | solution.py:13
  608.7 21.2 %collective-permute-start.40 = (bf16[16,1,10,128]{3,0,2,1:T(8,128)(2,1)S(1)}, bf16[16,1,10,128]{3,0,2,1:T(8,128)(2,1)S(1)}, u32[]{:S(2)}, u32[]{:S(2)}) collective-permute-start(bf16[16,1,10,128]{3,0,2,1:T(8,128)(2,1)S(1)} %get-tuple-element.52), channel_id=1, source_target_pairs={{0,16},{16,32},{32,48},{48,64},{64,80},{80,96},{96,112},{112,128},... | collective-permute-start | bytes 122888 | tf_op jit(solution)/shard_map/ppermute | solution.py:38
  634.5 4.6 collective-permute-done.41
  (227 shorter events, 146.6 us)
Async XLA Ops:
  1.5 12.9 %collective-permute-start = (bf16[16,1,8,128]{3,0,2,1:T(8,128)(2,1)S(1)}, bf16[16,1,8,128]{3,0,2,1:T(8,128)(2,1)S(1)}, u32[]{:S(2)}, u32[]{:S(2)}) collective-permute-start(bf16[16,1,8,128]{3,0,2,1:T(8,128)(2,1)S(1)} %copy.83), channel_id=1, source_target_pairs={{0,16},{16,32},{32,48},{48,64},{64,80},{80,96},{96,112},{112,128},... | collective-permute-start | bytes 98312 | tf_op jit(solution)/shard_map/ppermute | solution.py:25
  11.7 9.1 %collective-permute-start.1 = (bf16[16,1,8,128]{3,0,2,1:T(8,128)(2,1)S(1)}, bf16[16,1,8,128]{3,0,2,1:T(8,128)(2,1)S(1)}, u32[]{:S(2)}, u32[]{:S(2)}) collective-permute-start(bf16[16,1,8,128]{3,0,2,1:T(8,128)(2,1)S(1)} %copy.84), channel_id=1, source_target_pairs={{16,0},{32,16},{48,32},{64,48},{80,64},{96,80},{112,96},{128,112},... | collective-permute-start | bytes 98312 | tf_op jit(solution)/shard_map/ppermute | solution.py:26
  20.9 13.9 %collective-permute-start.2 = (bf16[16,6,1,128]{3,0,2,1:T(8,128)(2,1)S(1)}, bf16[16,6,1,128]{3,0,2,1:T(8,128)(2,1)S(1)}, u32[]{:S(2)}, u32[]{:S(2)}) collective-permute-start(bf16[16,6,1,128]{3,0,2,1:T(8,128)(2,1)S(1)} %get-tuple-element.62), channel_id=1, source_target_pairs={{0,1},{1,2},{2,3},{3,4},{4,5},{5,6},{6,7},{7,8},{8,9},{9,10},{10,1... | collective-permute-start | bytes 73736 | tf_op jit(solution)/shard_map/ppermute | solution.py:25
  24.0 10.8 %collective-permute-start.3 = (bf16[16,6,1,128]{3,0,2,1:T(8,128)(2,1)S(1)}, bf16[16,6,1,128]{3,0,2,1:T(8,128)(2,1)S(1)}, u32[]{:S(2)}, u32[]{:S(2)}) collective-permute-start(bf16[16,6,1,128]{3,0,2,1:T(8,128)(2,1)S(1)} %get-tuple-element.63), channel_id=1, source_target_pairs={{1,0},{2,1},{3,2},{4,3},{5,4},{6,5},{7,6},{8,7},{9,8},{10,9},{11,1... | collective-permute-start | bytes 73736 | tf_op jit(solution)/shard_map/ppermute | solution.py:26
  25.3 33.3 %collective-permute-start.8 = (f32[1,8,128]{2,1,0:T(8,128)S(1)}, f32[1,8,128]{2,1,0:T(8,128)S(1)}, u32[]{:S(2)}, u32[]{:S(2)}) collective-permute-start(f32[1,8,128]{2,1,0:T(8,128)S(1)} %get-tuple-element.117), channel_id=1, source_target_pairs={{16,0},{32,16},{48,32},{64,48},{80,64},{96,80},{112,96},{128,112},... | collective-permute-start | bytes 12296 | tf_op jit(solution)/shard_map/ppermute | solution.py:26
  27.2 31.4 %collective-permute-start.9 = (f32[1,8,128]{2,1,0:T(8,128)S(1)}, f32[1,8,128]{2,1,0:T(8,128)S(1)}, u32[]{:S(2)}, u32[]{:S(2)}) collective-permute-start(f32[1,8,128]{2,1,0:T(8,128)S(1)} %get-tuple-element.116), channel_id=1, source_target_pairs={{0,16},{16,32},{32,48},{48,64},{64,80},{80,96},{96,112},{112,128},... | collective-permute-start | bytes 12296 | tf_op jit(solution)/shard_map/ppermute | solution.py:25
  53.1 11.5 %collective-permute-start.4 = (bf16[16,1,8,128]{3,0,2,1:T(8,128)(2,1)S(1)}, bf16[16,1,8,128]{3,0,2,1:T(8,128)(2,1)S(1)}, u32[]{:S(2)}, u32[]{:S(2)}) collective-permute-start(bf16[16,1,8,128]{3,0,2,1:T(8,128)(2,1)S(1)} %get-tuple-element.68), channel_id=1, source_target_pairs={{0,16},{16,32},{32,48},{48,64},{64,80},{80,96},{96,112},{112,128},... | collective-permute-start | bytes 98312 | tf_op jit(solution)/shard_map/ppermute | solution.py:25
  56.7 9.1 %collective-permute-start.5 = (bf16[16,1,8,128]{3,0,2,1:T(8,128)(2,1)S(1)}, bf16[16,1,8,128]{3,0,2,1:T(8,128)(2,1)S(1)}, u32[]{:S(2)}, u32[]{:S(2)}) collective-permute-start(bf16[16,1,8,128]{3,0,2,1:T(8,128)(2,1)S(1)} %get-tuple-element.69), channel_id=1, source_target_pairs={{16,0},{32,16},{48,32},{64,48},{80,64},{96,80},{112,96},{128,112},... | collective-permute-start | bytes 98312 | tf_op jit(solution)/shard_map/ppermute | solution.py:26
  58.6 12.6 %collective-permute-start.10 = (f32[6,1,128]{2,1,0:T(1,128)S(1)}, f32[6,1,128]{2,1,0:T(1,128)S(1)}, u32[]{:S(2)}, u32[]{:S(2)}) collective-permute-start(f32[6,1,128]{2,1,0:T(1,128)S(1)} %get-tuple-element.102), channel_id=1, source_target_pairs={{1,0},{2,1},{3,2},{4,3},{5,4},{6,5},{7,6},{8,7},{9,8},{10,9},{11,1... | collective-permute-start | bytes 9224 | tf_op jit(solution)/shard_map/ppermute | solution.py:26
  59.9 11.4 %collective-permute-start.11 = (f32[6,1,128]{2,1,0:T(1,128)S(1)}, f32[6,1,128]{2,1,0:T(1,128)S(1)}, u32[]{:S(2)}, u32[]{:S(2)}) collective-permute-start(f32[6,1,128]{2,1,0:T(1,128)S(1)} %get-tuple-element.101), channel_id=1, source_target_pairs={{0,1},{1,2},{2,3},{3,4},{4,5},{5,6},{6,7},{7,8},{8,9},{9,10},{10,1... | collective-permute-start | bytes 9224 | tf_op jit(solution)/shard_map/ppermute | solution.py:25
  95.1 9.8 %collective-permute-start.12 = (f32[1,8,128]{2,1,0:T(8,128)S(1)}, f32[1,8,128]{2,1,0:T(8,128)S(1)}, u32[]{:S(2)}, u32[]{:S(2)}) collective-permute-start(f32[1,8,128]{2,1,0:T(8,128)S(1)} %get-tuple-element.115), channel_id=1, source_target_pairs={{16,0},{32,16},{48,32},{64,48},{80,64},{96,80},{112,96},{128,112},... | collective-permute-start | bytes 12296 | tf_op jit(solution)/shard_map/ppermute | solution.py:26
  97.0 8.7 %collective-permute-start.13 = (f32[1,8,128]{2,1,0:T(8,128)S(1)}, f32[1,8,128]{2,1,0:T(8,128)S(1)}, u32[]{:S(2)}, u32[]{:S(2)}) collective-permute-start(f32[1,8,128]{2,1,0:T(8,128)S(1)} %get-tuple-element.114), channel_id=1, source_target_pairs={{0,16},{16,32},{32,48},{48,64},{64,80},{80,96},{96,112},{112,128},... | collective-permute-start | bytes 12296 | tf_op jit(solution)/shard_map/ppermute | solution.py:25
  105.7 6.1 collective-permute-start.14
  112.7 10.9 %collective-permute-start.16 = (f32[1,8,128]{2,1,0:T(8,128)S(1)}, f32[1,8,128]{2,1,0:T(8,128)S(1)}, u32[]{:S(2)}, u32[]{:S(2)}) collective-permute-start(f32[1,8,128]{2,1,0:T(8,128)S(1)} %get-tuple-element.113), channel_id=1, source_target_pairs={{16,0},{32,16},{48,32},{64,48},{80,64},{96,80},{112,96},{128,112},... | collective-permute-start | bytes 12296 | tf_op jit(solution)/shard_map/ppermute | solution.py:26
  114.7 9.7 %collective-permute-start.17 = (f32[1,8,128]{2,1,0:T(8,128)S(1)}, f32[1,8,128]{2,1,0:T(8,128)S(1)}, u32[]{:S(2)}, u32[]{:S(2)}) collective-permute-start(f32[1,8,128]{2,1,0:T(8,128)S(1)} %get-tuple-element.112), channel_id=1, source_target_pairs={{0,16},{16,32},{32,48},{48,64},{64,80},{80,96},{96,112},{112,128},... | collective-permute-start | bytes 12296 | tf_op jit(solution)/shard_map/ppermute | solution.py:25
  131.2 10.9 %collective-permute-start.20 = (f32[1,8,128]{2,1,0:T(8,128)S(1)}, f32[1,8,128]{2,1,0:T(8,128)S(1)}, u32[]{:S(2)}, u32[]{:S(2)}) collective-permute-start(f32[1,8,128]{2,1,0:T(8,128)S(1)} %get-tuple-element.111), channel_id=1, source_target_pairs={{16,0},{32,16},{48,32},{64,48},{80,64},{96,80},{112,96},{128,112},... | collective-permute-start | bytes 12296 | tf_op jit(solution)/shard_map/ppermute | solution.py:26
  133.1 9.7 %collective-permute-start.21 = (f32[1,8,128]{2,1,0:T(8,128)S(1)}, f32[1,8,128]{2,1,0:T(8,128)S(1)}, u32[]{:S(2)}, u32[]{:S(2)}) collective-permute-start(f32[1,8,128]{2,1,0:T(8,128)S(1)} %get-tuple-element.110), channel_id=1, source_target_pairs={{0,16},{16,32},{32,48},{48,64},{64,80},{80,96},{96,112},{112,128},... | collective-permute-start | bytes 12296 | tf_op jit(solution)/shard_map/ppermute | solution.py:25
  142.8 6.5 %collective-permute-start.22 = (f32[6,1,128]{2,1,0:T(1,128)S(1)}, f32[6,1,128]{2,1,0:T(1,128)S(1)}, u32[]{:S(2)}, u32[]{:S(2)}) collective-permute-start(f32[6,1,128]{2,1,0:T(1,128)S(1)} %get-tuple-element.96), channel_id=1, source_target_pairs={{1,0},{2,1},{3,2},{4,3},{5,4},{6,5},{7,6},{8,7},{9,8},{10,9},{11,1... | collective-permute-start | bytes 9224 | tf_op jit(solution)/shard_map/ppermute | solution.py:26
  151.2 10.9 %collective-permute-start.24 = (bf16[1,10,128]{2,1,0:T(8,128)(2,1)S(1)}, bf16[1,10,128]{2,1,0:T(8,128)(2,1)S(1)}, u32[]{:S(2)}, u32[]{:S(2)}) collective-permute-start(bf16[1,10,128]{2,1,0:T(8,128)(2,1)S(1)} %get-tuple-element.88), channel_id=1, source_target_pairs={{0,16},{16,32},{32,48},{48,64},{64,80},{80,96},{96,112},{112,128},... | collective-permute-start | bytes 7688 | tf_op jit(solution)/shard_map/ppermute | solution.py:38
  160.2 8.8 %collective-permute-start.25 = (bf16[1,10,128]{2,1,0:T(8,128)(2,1)S(1)}, bf16[1,10,128]{2,1,0:T(8,128)(2,1)S(1)}, u32[]{:S(2)}, u32[]{:S(2)}) collective-permute-start(bf16[1,10,128]{2,1,0:T(8,128)(2,1)S(1)} %get-tuple-element.89), channel_id=1, source_target_pairs={{16,0},{32,16},{48,32},{64,48},{80,64},{96,80},{112,96},{128,112},... | collective-permute-start | bytes 7688 | tf_op jit(solution)/shard_map/ppermute | solution.py:38
  169.1 7.1 %collective-permute-start.26 = (bf16[4,1,128]{2,1,0:T(2,128)(2,1)S(1)}, bf16[4,1,128]{2,1,0:T(2,128)(2,1)S(1)}, u32[]{:S(2)}, u32[]{:S(2)}) collective-permute-start(bf16[4,1,128]{2,1,0:T(2,128)(2,1)S(1)} %get-tuple-element.107), channel_id=1, source_target_pairs={{0,1},{1,2},{2,3},{3,4},{4,5},{5,6},{6,7},{7,8},{8,9},{9,10},{10,1... | collective-permute-start | bytes 3080 | tf_op jit(solution)/shard_map/ppermute | solution.py:38
  174.9 7.0 %collective-permute-start.27 = (bf16[4,1,128]{2,1,0:T(2,128)(2,1)S(1)}, bf16[4,1,128]{2,1,0:T(2,128)(2,1)S(1)}, u32[]{:S(2)}, u32[]{:S(2)}) collective-permute-start(bf16[4,1,128]{2,1,0:T(2,128)(2,1)S(1)} %get-tuple-element.108), channel_id=1, source_target_pairs={{1,0},{2,1},{3,2},{4,3},{5,4},{6,5},{7,6},{8,7},{9,8},{10,9},{11,1... | collective-permute-start | bytes 3080 | tf_op jit(solution)/shard_map/ppermute | solution.py:38
  185.8 8.8 %collective-permute-start.29 = (bf16[1,10,128]{2,1,0:T(8,128)(2,1)S(1)}, bf16[1,10,128]{2,1,0:T(8,128)(2,1)S(1)}, u32[]{:S(2)}, u32[]{:S(2)}) collective-permute-start(bf16[1,10,128]{2,1,0:T(8,128)(2,1)S(1)} %get-tuple-element.87), channel_id=1, source_target_pairs={{16,0},{32,16},{48,32},{64,48},{80,64},{96,80},{112,96},{128,112},... | collective-permute-start | bytes 7688 | tf_op jit(solution)/shard_map/ppermute | solution.py:38
  194.7 7.3 %collective-permute-start.30 = (bf16[4,1,128]{2,1,0:T(2,128)(2,1)S(1)}, bf16[4,1,128]{2,1,0:T(2,128)(2,1)S(1)}, u32[]{:S(2)}, u32[]{:S(2)}) collective-permute-start(bf16[4,1,128]{2,1,0:T(2,128)(2,1)S(1)} %get-tuple-element.105), channel_id=1, source_target_pairs={{0,1},{1,2},{2,3},{3,4},{4,5},{5,6},{6,7},{7,8},{8,9},{9,10},{10,1... | collective-permute-start | bytes 3080 | tf_op jit(solution)/shard_map/ppermute | solution.py:38
  200.7 7.0 %collective-permute-start.31 = (bf16[4,1,128]{2,1,0:T(2,128)(2,1)S(1)}, bf16[4,1,128]{2,1,0:T(2,128)(2,1)S(1)}, u32[]{:S(2)}, u32[]{:S(2)}) collective-permute-start(bf16[4,1,128]{2,1,0:T(2,128)(2,1)S(1)} %get-tuple-element.106), channel_id=1, source_target_pairs={{1,0},{2,1},{3,2},{4,3},{5,4},{6,5},{7,6},{8,7},{9,8},{10,9},{11,1... | collective-permute-start | bytes 3080 | tf_op jit(solution)/shard_map/ppermute | solution.py:38
  211.6 8.8 %collective-permute-start.33 = (bf16[1,10,128]{2,1,0:T(8,128)(2,1)S(1)}, bf16[1,10,128]{2,1,0:T(8,128)(2,1)S(1)}, u32[]{:S(2)}, u32[]{:S(2)}) collective-permute-start(bf16[1,10,128]{2,1,0:T(8,128)(2,1)S(1)} %get-tuple-element.85), channel_id=1, source_target_pairs={{16,0},{32,16},{48,32},{64,48},{80,64},{96,80},{112,96},{128,112},... | collective-permute-start | bytes 7688 | tf_op jit(solution)/shard_map/ppermute | solution.py:38
  221.7 24.3 %collective-permute-start.34 = (bf16[4,1,128]{2,1,0:T(2,128)(2,1)}, bf16[4,1,128]{2,1,0:T(2,128)(2,1)}, u32[]{:S(2)}, u32[]{:S(2)}) collective-permute-start(bf16[4,1,128]{2,1,0:T(2,128)(2,1)} %get-tuple-element.103), channel_id=1, source_target_pairs={{0,1},{1,2},{2,3},{3,4},{4,5},{5,6},{6,7},{7,8},{8,9},{9,10},{10,1... | collective-permute-start | bytes 3080 | tf_op jit(solution)/shard_map/ppermute | solution.py:38
  228.1 18.0 %collective-permute-start.35 = (bf16[4,1,128]{2,1,0:T(2,128)(2,1)}, bf16[4,1,128]{2,1,0:T(2,128)(2,1)}, u32[]{:S(2)}, u32[]{:S(2)}) collective-permute-start(bf16[4,1,128]{2,1,0:T(2,128)(2,1)} %get-tuple-element.104), channel_id=1, source_target_pairs={{1,0},{2,1},{3,2},{4,3},{5,4},{6,5},{7,6},{8,7},{9,8},{10,9},{11,1... | collective-permute-start | bytes 3080 | tf_op jit(solution)/shard_map/ppermute | solution.py:38
  273.8 34.4 %collective-permute-start.36 = (bf16[16,1,10,128]{3,0,2,1:T(8,128)(2,1)S(1)}, bf16[16,1,10,128]{3,0,2,1:T(8,128)(2,1)S(1)}, u32[]{:S(2)}, u32[]{:S(2)}) collective-permute-start(bf16[16,1,10,128]{3,0,2,1:T(8,128)(2,1)S(1)} %get-tuple-element.54), channel_id=1, source_target_pairs={{0,16},{16,32},{32,48},{48,64},{64,80},{80,96},{96,112},{112,128},... | collective-permute-start | bytes 122888 | tf_op jit(solution)/shard_map/ppermute | solution.py:38
  276.1 32.1 %collective-permute-start.37 = (bf16[16,1,10,128]{3,0,2,1:T(8,128)(2,1)S(1)}, bf16[16,1,10,128]{3,0,2,1:T(8,128)(2,1)S(1)}, u32[]{:S(2)}, u32[]{:S(2)}) collective-permute-start(bf16[16,1,10,128]{3,0,2,1:T(8,128)(2,1)S(1)} %get-tuple-element.55), channel_id=1, source_target_pairs={{16,0},{32,16},{48,32},{64,48},{80,64},{96,80},{112,96},{128,112},... | collective-permute-start | bytes 122888 | tf_op jit(solution)/shard_map/ppermute | solution.py:38
  608.7 25.8 %collective-permute-start.40 = (bf16[16,1,10,128]{3,0,2,1:T(8,128)(2,1)S(1)}, bf16[16,1,10,128]{3,0,2,1:T(8,128)(2,1)S(1)}, u32[]{:S(2)}, u32[]{:S(2)}) collective-permute-start(bf16[16,1,10,128]{3,0,2,1:T(8,128)(2,1)S(1)} %get-tuple-element.52), channel_id=1, source_target_pairs={{0,16},{16,32},{32,48},{48,64},{64,80},{80,96},{96,112},{112,128},... | collective-permute-start | bytes 122888 | tf_op jit(solution)/shard_map/ppermute | solution.py:38
  629.9 9.2 %collective-permute-start.41 = (bf16[16,1,10,128]{3,0,2,1:T(8,128)(2,1)S(1)}, bf16[16,1,10,128]{3,0,2,1:T(8,128)(2,1)S(1)}, u32[]{:S(2)}, u32[]{:S(2)}) collective-permute-start(bf16[16,1,10,128]{3,0,2,1:T(8,128)(2,1)S(1)} %get-tuple-element.53), channel_id=1, source_target_pairs={{16,0},{32,16},{48,32},{64,48},{80,64},{96,80},{112,96},{128,112},... | collective-permute-start | bytes 122888 | tf_op jit(solution)/shard_map/ppermute | solution.py:38
  (38 other events, 980.7 us)
